TPU v7x, 32 devices: a whole 2x2x4 slice. The times are simulated.
32 devices in a mesh: feat: 8 (over z, core), col: 4 (over y, x).
Axes of the slice: x: 2, y: 2, z: 4, core: 2. Of those that a mesh axis runs over, the one named last changes fastest.
Arguments:
- self_feats: bfloat16 [4096, 128], P(('feat', 'col')), may hold values from -6 to 6
- neighbour_feats: bfloat16 [128, 16384], P('feat', 'col'), may hold values from -6 to 6
- tiles: bfloat16 [1024, 128, 128], P('col'), may hold values from 0 to 1, as said below
- tile_rows: int32 [1024], P('col'), may hold values from 0 to 31, as said below
- tile_cols: int32 [1024], P('col'), may hold values from 0 to 31
- tile_count: int32 [4], P('col'), may hold values from 1 to 256, 768 in all
- owner_order: int32 [32], replicated, may hold values from 0 to 31, as said below
- degree: int32 [4096], P(('feat', 'col')), may hold values from 64 to 192
- w_self: bfloat16 [128, 256], replicated, may hold values from -0.5 to 0.5
- w_neigh: bfloat16 [128, 256], replicated, may hold values from -0.5 to 0.5
- bias: float32 [256], replicated, may hold values from -3 to 3
- upstream: bfloat16 [4096, 256], P(('feat', 'col')), may hold values from -6 to 6
Outputs:
- hidden_out: bfloat16 [4096, 256], P(('feat', 'col'))
- neigh_grad: bfloat16 [128, 16384], P('feat', 'col')
Inputs may be any that keep to these rules, and one draw needn't show every extreme that they name: `tiles`: every entry is 0 or 1. `tile_count`: slots at or after a group's count are ignored; some group has all 256 slots live. `owner_order`: a permutation of the row blocks. `tile_rows`: in every column group, slot s has a row block whose owner position p satisfies (p) % 4 == s % 4.
All inputs are finite; a program needn't handle non-finite values.
Results may differ from a plain program's by a relative error of at most 0.0065.
Values may be sent and summed in bfloat16 or wider, within the bound.
No kernel may reach another device: no remote copies, remote signals or barrier semaphores. Data moves between devices by JAX's collectives and lax.ppermute only.
A program may use at most 64 MiB of HBM per device.

v0:
```python
import jax
import jax.numpy as jnp
from jax import lax
from jax.sharding import PartitionSpec as P


def local(
    self_feats,
    neighbour_feats,
    tiles,
    tile_rows,
    tile_cols,
    tile_count,
    owner_order,
    degree,
    w_self,
    w_neigh,
    bias,
    upstream,
):
    nfeat = lax.axis_size("feat")
    ncol = lax.axis_size("col")
    slots, tile_size, _ = tiles.shape
    slice_width = neighbour_feats.shape[0]
    col_blocks = neighbour_feats.shape[1] // tile_size
    row_blocks = self_feats.shape[0] // tile_size
    blocks_total = owner_order.shape[0]
    places = (
        jnp.zeros((blocks_total,), jnp.int32)
        .at[owner_order]
        .set(jnp.arange(blocks_total, dtype=jnp.int32))
    )
    target = places[tile_rows]
    live = (jnp.arange(slots, dtype=jnp.int32) < tile_count[0]).astype(jnp.float32)
    blocked = neighbour_feats.reshape(slice_width, col_blocks, tile_size).transpose(1, 0, 2)
    picked = blocked[tile_cols]
    products = (
        jnp.einsum("nfk,nrk->nfr", picked, tiles, preferred_element_type=jnp.float32)
        * live[:, None, None]
    )
    partial_value = (
        jnp.zeros((blocks_total, slice_width, tile_size), jnp.float32).at[target].add(products)
    )
    grid = partial_value.reshape(nfeat, ncol, row_blocks, slice_width, tile_size)
    total = lax.psum(grid, "col")
    mine = lax.dynamic_slice_in_dim(total, lax.axis_index("col"), 1, 1)
    owned = lax.all_to_all(mine, "feat", split_axis=0, concat_axis=1, tiled=True)
    summed = owned.reshape(nfeat, row_blocks, slice_width, tile_size).transpose(1, 3, 0, 2)
    summed = summed.reshape(row_blocks * tile_size, nfeat * slice_width)
    scale = lax.rsqrt(degree.astype(jnp.float32))[:, None]
    aggregate = (summed * scale).astype(jnp.bfloat16)
    pre = jnp.dot(self_feats, w_self, preferred_element_type=jnp.float32)
    pre = pre + jnp.dot(aggregate, w_neigh, preferred_element_type=jnp.float32) + bias
    gate = jax.nn.sigmoid(pre)
    hidden_out = (pre * gate).astype(jnp.bfloat16)
    slope = gate * (1.0 + pre * (1.0 - gate))
    dpre = (upstream.astype(jnp.float32) * slope).astype(jnp.bfloat16)
    dagg = lax.dot_general(
        dpre, w_neigh, (((1,), (1,)), ((), ())), preferred_element_type=jnp.float32
    )
    back = (dagg * scale).astype(jnp.bfloat16)
    arranged = back.reshape(row_blocks, tile_size, nfeat, slice_width).transpose(2, 0, 3, 1)
    arranged = arranged.reshape(nfeat, 1, row_blocks, slice_width, tile_size)
    regrouped = lax.all_to_all(arranged, "feat", split_axis=0, concat_axis=0, tiled=True)
    everything = lax.all_gather(regrouped, "col", axis=1, tiled=True)
    row_grads = everything.reshape(blocks_total, slice_width, tile_size)
    taken = row_grads[target]
    pieces = (
        jnp.einsum("nfr,nrk->nfk", taken, tiles, preferred_element_type=jnp.float32)
        * live[:, None, None]
    )
    onehot_cols = (tile_cols[:, None] == jnp.arange(col_blocks, dtype=jnp.int32)[None, :]).astype(
        jnp.float32
    )
    col_total = jnp.einsum("nc,nfk->fck", onehot_cols, pieces, precision=lax.Precision.HIGHEST)
    neigh_grad = col_total.reshape(slice_width, col_blocks * tile_size).astype(jnp.bfloat16)
    return (hidden_out, neigh_grad)


def solution(mesh):
    in_specs = (
        P(("feat", "col"), None),
        P("feat", "col"),
        P("col", None, None),
        P("col"),
        P("col"),
        P("col"),
        P(),
        P(("feat", "col")),
        P(),
        P(),
        P(),
        P(("feat", "col"), None),
    )
    out_specs = (P(("feat", "col"), None), P("feat", "col"))
    return jax.shard_map(local, mesh=mesh, in_specs=in_specs, out_specs=out_specs, check_vma=False)
```

profile of v0, /device:TPU:0, one launch (start us, length us, event | category | flops | bytes accessed | tf_op | source)
XLA Modules:
  0.0 141.6 jit_solution(16048866213782390295)
XLA Ops:
  7.2 0.7 compare_select_fusion.3
  7.9 0.7 scatter_custom_fusion
  8.6 0.7 fusion.14
  9.3 0.7 fusion.15
  10.0 20.7 %compare_select_fusion.4 = s32[256]{0:T(256)S(1)} fusion(s32[256]{0:T(256)} %param.15, s32[]{:T(128)} %bitcast, s32[]{:T(128)} %bitcast.1, s32[]{:T(128)} %bitcast.2, s32[]{:T(128)} %bitcast.3, s32[]{:T(128)} %bitcast.4, s32[]{:T(128)} %bitcast.5, s32[]{:T(128)} %bitcast.6, s32[]{:T(128)} %bitcast.7, s32[]{:T(128)} %bitcast.8, s32[]{:T(128)} %bitcast.9, ...), kind=kLoop, calls=%fused_computation.30 | loop fusion | flops 16640 | bytes 2176 | tf_op jit(solution)/shard_map/gather | solution.py:33
  31.5 0.7 compare_select_fusion.1
  32.2 0.8 gather_fusion
  33.0 6.8 %convolution_multiply_fusion.1 = f32[256,16,128]{2,1,0:T(8,128)S(1)} fusion(bf16[256,16,128]{2,1,0:T(8,128)(2,1)S(1)} %gather_fusion, bf16[256,128,128]{2,1,0:T(8,128)(2,1)} %param.14, f32[256]{0:T(256)S(1)} %compare_convert_fusion), kind=kOutput, calls=%fused_computation.7 | convolution fusion | flops 134742016 | bytes 11535360 | tf_op jit(solution)/shard_map/nfk,nrk->nfr/dot_general | solution.py:38
  39.9 9.0 %scatter_fusion = f32[32,16,128]{2,1,0:T(8,128)S(1)} fusion(f32[32,16,128]{2,1,0:T(8,128)S(1)} %broadcast_in_dim.8, s32[256]{0:T(256)S(1)} %bitcast.83, f32[256,16,128]{2,1,0:T(8,128)S(1)} %convolution_multiply_fusion.1), kind=kCustom, calls=%fused_computation.3 | custom fusion | flops 524288 | bytes 6292480 | tf_op jit(solution)/shard_map/scatter-add | solution.py:42
  48.9 0.7 copy-done.1
  49.6 0.1 fusion.16
  49.8 45.6 %all-reduce.2.cloned.1.call-done = f32[8,4,1,16,128]{4,3,1,0,2:T(8,128)} async-done(((f32[8,4,1,16,128]{4,3,1,0,2:T(8,128)}), f32[8,4,1,16,128]{4,3,1,0,2:T(8,128)}) %all-reduce.2.cloned.1.call-update) | async-done | bytes 262160 | tf_op jit(solution)/shard_map/psum | solution.py:45
  95.4 1.5 %dynamic-slice_bitcast_fusion = f32[8,1,1,16,128]{4,3,1,2,0:T(8,128)} fusion(f32[8,4,1,16,128]{4,3,1,0,2:T(8,128)} %all-reduce.2.cloned.1.call-done, s32[]{:T(128)S(6)} %select_n.27), kind=kLoop, calls=%fused_computation.20 | loop fusion | bytes 131076 | tf_op jit(solution)/shard_map/dynamic_slice | solution.py:46
  96.9 4.6 %all-to-all-start = ((f32[8,1,1,16,128]{4,3,1,2,0:T(8,128)}), f32[8,1,1,16,128]{4,3,1,2,0:T(8,128)S(1)}, u32[]{:S(2)}, u32[]{:S(2)}) async-start(f32[8,1,1,16,128]{4,3,1,2,0:T(8,128)} %dynamic-slice_bitcast_fusion), calls=%async_computation | async-start | bytes 131072 | tf_op jit(solution)/shard_map/all_to_all | solution.py:47
  101.5 5.9 %all-to-all-done = f32[8,1,1,16,128]{4,3,1,2,0:T(8,128)S(1)} async-done(((f32[8,1,1,16,128]{4,3,1,2,0:T(8,128)}), f32[8,1,1,16,128]{4,3,1,2,0:T(8,128)S(1)}, u32[]{:S(2)}, u32[]{:S(2)}) %all-to-all-start) | async-done | bytes 65568 | tf_op jit(solution)/shard_map/all_to_all | solution.py:47
  107.4 0.9 multiply_convert_fusion.1
  108.3 0.8 fusion.6
  109.1 3.3 %all-to-all-start.1 = ((bf16[8,1,1,16,128]{4,3,1,2,0:T(8,128)(2,1)}), bf16[8,1,1,16,128]{4,3,1,2,0:T(8,128)(2,1)S(1)}, u32[]{:S(2)}, u32[]{:S(2)}) async-start(bf16[8,1,1,16,128]{4,3,1,2,0:T(8,128)(2,1)} %bitcast.43), calls=%async_computation.1 | async-start | bytes 65536 | tf_op jit(solution)/shard_map/all_to_all | solution.py:64
  112.5 5.7 %all-to-all-done.1 = bf16[8,1,1,16,128]{4,3,1,2,0:T(8,128)(2,1)S(1)} async-done(((bf16[8,1,1,16,128]{4,3,1,2,0:T(8,128)(2,1)}), bf16[8,1,1,16,128]{4,3,1,2,0:T(8,128)(2,1)S(1)}, u32[]{:S(2)}, u32[]{:S(2)}) %all-to-all-start.1) | async-done | bytes 32800 | tf_op jit(solution)/shard_map/all_to_all | solution.py:64
  118.1 8.9 %all_gather.3 = bf16[8,4,1,16,128]{4,3,1,0,2:T(8,128)(2,1)S(1)} all-gather(bf16[8,1,1,16,128]{4,3,1,0,2:T(8,128)(2,1)S(1)} %bitcast.81), channel_id=1, replica_groups=mesh['feat'=8,'col'=4] {'col'}, dimensions={1}, use_global_device_ids=true | all-gather | bytes 163840 | tf_op jit(solution)/shard_map/all_gather | solution.py:65
  127.1 0.8 gather_fusion.1
  127.9 4.7 %convolution_multiply_fusion = f32[256,16,128]{2,1,0:T(8,128)S(1)} fusion(bf16[256,16,128]{2,1,0:T(8,128)(2,1)S(1)} %gather_fusion.1, bf16[256,128,128]{2,1,0:T(8,128)(2,1)} %param.14, f32[256]{0:T(256)S(1)} %compare_convert_fusion), kind=kOutput, calls=%fused_computation.6 | convolution fusion | flops 134742016 | bytes 11535360 | tf_op jit(solution)/shard_map/nfr,nrk->nfk/dot_general | solution.py:69
  132.6 1.4 fusion.2
  134.0 0.7 copy.30
  (28 shorter events, 0.2 us)
Async XLA Ops:
  7.2 24.3 %copy-start = (bf16[16,4096]{1,0:T(8,128)(2,1)S(1)}, bf16[16,4096]{1,0:T(8,128)(2,1)}, u32[]{:S(2)}) copy-start(bf16[16,4096]{1,0:T(8,128)(2,1)} %param.13) | copy-start | bytes 393220
  7.2 88.2 %all-reduce.2.cloned.1.call-start = ((), (), s32[]{:S(2)}) async-start(), calls=%async_computation.2 | async-start | bytes 524288 | tf_op jit(solution)/shard_map/psum | solution.py:45
  39.9 9.8 %copy-start.2 = (bf16[128,256]{1,0:T(8,128)(2,1)S(1)}, bf16[128,256]{1,0:T(8,128)(2,1)}, u32[]{:S(2)}) copy-start(bf16[128,256]{1,0:T(8,128)(2,1)} %param.20) | copy-start | bytes 196612
  39.9 9.8 %copy-start.3 = (bf16[128,128]{1,0:T(8,128)(2,1)S(1)}, bf16[128,128]{1,0:T(8,128)(2,1)}, u32[]{:S(2)}) copy-start(bf16[128,128]{1,0:T(8,128)(2,1)} %param.12) | copy-start | bytes 98308
  39.9 61.6 %copy-start.8 = (s32[128]{0:T(128)S(1)}, s32[128]{0:T(128)}, u32[]{:S(2)}) copy-start(s32[128]{0:T(128)} %param.19) | copy-start | bytes 1540
  39.9 67.5 %copy-start.5 = (bf16[128,256]{1,0:T(8,128)(2,1)S(1)}, bf16[128,256]{1,0:T(8,128)(2,1)}, u32[]{:S(2)}) copy-start(bf16[128,256]{1,0:T(8,128)(2,1)} %param.21) | copy-start | bytes 196612
  39.9 67.5 %copy-start.7 = (f32[256]{0:T(256)S(1)}, f32[256]{0:T(256)}, u32[]{:S(2)}) copy-start(f32[256]{0:T(256)} %param.22) | copy-start | bytes 3076
  39.9 68.4 %copy-start.6 = (bf16[128,256]{1,0:T(8,128)(2,1)S(1)}, bf16[128,256]{1,0:T(8,128)(2,1)}, u32[]{:S(2)}) copy-start(bf16[128,256]{1,0:T(8,128)(2,1)} %param.23) | copy-start | bytes 196612
  48.9 0.7 copy-start.1
  96.9 10.5 %all-to-all-start = ((f32[8,1,1,16,128]{4,3,1,2,0:T(8,128)}), f32[8,1,1,16,128]{4,3,1,2,0:T(8,128)S(1)}, u32[]{:S(2)}, u32[]{:S(2)}) async-start(f32[8,1,1,16,128]{4,3,1,2,0:T(8,128)} %dynamic-slice_bitcast_fusion), calls=%async_computation | async-start | bytes 131072 | tf_op jit(solution)/shard_map/all_to_all | solution.py:47
  109.1 9.0 %all-to-all-start.1 = ((bf16[8,1,1,16,128]{4,3,1,2,0:T(8,128)(2,1)}), bf16[8,1,1,16,128]{4,3,1,2,0:T(8,128)(2,1)S(1)}, u32[]{:S(2)}, u32[]{:S(2)}) async-start(bf16[8,1,1,16,128]{4,3,1,2,0:T(8,128)(2,1)} %bitcast.43), calls=%async_computation.1 | async-start | bytes 65536 | tf_op jit(solution)/shard_map/all_to_all | solution.py:64
  127.9 4.7 %copy-start.4 = (s32[256]{0:T(256)S(1)}, s32[256]{0:T(256)}, u32[]{:S(2)}) copy-start(s32[256]{0:T(256)} %param.16) | copy-start | bytes 3076
Sparse Core Ops, SparseCore 0:
  49.7 45.6 all-reduce.1
where the time goes:
time: 142 us
  waiting for transfers between devices  57.2 us (40%)
  other arithmetic  31.1 us (22%)
  between operations  14.9 us (10%)
  matrix products  14.7 us (10%)
  blocking collectives  8.92 us (6%)
  starting transfers between devices  7.98 us (6%)
  local copies, waits for them, and re-layouts  6.79 us (5%)
    psum x1, waiting for transfers between devices, local(): total = lax.psum(grid, 'col')  45.6 us
    gather x1, other arithmetic, local(): target = places[tile_rows]  20.7 us
    scatter-add x1, other arithmetic, local(): jnp.zeros((blocks_total, slice_width, tile_size), jnp.float32).at[target]  8.97 us
    all_gather x1, blocking collectives, local(): everything = lax.all_gather(regrouped, 'col', axis=1, tiled=True)  8.92 us
    dot_general x1, matrix products, local(): jnp.einsum('nfk,nrk->nfr', picked, tiles, preferred_element_type=jnp.floa...  6.77 us
    all_to_all x1, waiting for transfers between devices, local(): lax.all_to_all(mine, 'feat', split_axis=0, concat_axis=1, tiled=True)  5.9 us
    all_to_all x1, waiting for transfers between devices, local(): lax.all_to_all(arranged, 'feat', split_axis=0, concat_axis=0, tiled=True)  5.66 us
    dot_general x1, matrix products, local(): jnp.einsum('nfr,nrk->nfk', taken, tiles, preferred_element_type=jnp.float32)  4.68 us
  transfers between devices with their start and end apart: 3, of which 3 were waited for; matrix products, arithmetic and copies ran while one was open for 0% of the time, Pallas kernels for 0%

commit v1 on v0

--- a/solution.py
+++ b/solution.py
@@ -2,6 +2,7 @@
 import jax.numpy as jnp
 from jax import lax
 from jax.sharding import PartitionSpec as P
+from jax.lax import all_gather
 
 
 def local(
@@ -42,7 +43,8 @@
         jnp.zeros((blocks_total, slice_width, tile_size), jnp.float32).at[target].add(products)
     )
     grid = partial_value.reshape(nfeat, ncol, row_blocks, slice_width, tile_size)
-    total = lax.psum(grid, "col")
+    finish_desk_now = lambda x0: jnp.sum(all_gather(x0, "col"), axis=0)
+    total = finish_desk_now(grid)
     mine = lax.dynamic_slice_in_dim(total, lax.axis_index("col"), 1, 1)
     owned = lax.all_to_all(mine, "feat", split_axis=0, concat_axis=1, tiled=True)
     summed = owned.reshape(nfeat, row_blocks, slice_width, tile_size).transpose(1, 3, 0, 2)

time: 142 us -> 126 us (0.89)
  waiting for transfers between devices: 57.2 us -> 40.9 us
    psum x1 -> x0, waiting for transfers between devices: 45.6 us -> none  [local(): total = lax.psum(grid, 'col')]
    all_gather x0 -> x1, waiting for transfers between devices: none -> 29.3 us  [local(): finish_desk_now = lambda x0: jnp.sum(all_gather(x0, 'col'), axis=0)]
where the time goes in v1:
time: 126 us
  waiting for transfers between devices  40.9 us (32%)
  other arithmetic  32.4 us (26%)
  between operations  14.9 us (12%)
  matrix products  14.7 us (12%)
  blocking collectives  8.92 us (7%)
  starting transfers between devices  7.98 us (6%)
  local copies, waits for them, and re-layouts  5.93 us (5%)
    all_gather x1, waiting for transfers between devices, local(): finish_desk_now = lambda x0: jnp.sum(all_gather(x0, 'col'), axis=0)  29.3 us
    gather x1, other arithmetic, local(): target = places[tile_rows]  20.7 us
    scatter-add x1, other arithmetic, local(): jnp.zeros((blocks_total, slice_width, tile_size), jnp.float32).at[target]  8.97 us
    all_gather x1, blocking collectives, local(): everything = lax.all_gather(regrouped, 'col', axis=1, tiled=True)  8.92 us
    dot_general x1, matrix products, local(): jnp.einsum('nfk,nrk->nfr', picked, tiles, preferred_element_type=jnp.floa...  6.77 us
    all_to_all x1, waiting for transfers between devices, local(): lax.all_to_all(mine, 'feat', split_axis=0, concat_axis=1, tiled=True)  5.9 us
    all_to_all x1, waiting for transfers between devices, local(): lax.all_to_all(arranged, 'feat', split_axis=0, concat_axis=0, tiled=True)  5.66 us
    dot_general x1, matrix products, local(): jnp.einsum('nfr,nrk->nfk', taken, tiles, preferred_element_type=jnp.float32)  4.68 us
  transfers between devices with their start and end apart: 3, of which 3 were waited for; matrix products, arithmetic and copies ran while one was open for 0% of the time, Pallas kernels for 0%

profile of v1, /device:TPU:0, one launch (start us, length us, event | category | flops | bytes accessed | tf_op | source)
XLA Modules:
  0.0 125.7 jit_solution(18328865845129148251)
XLA Ops:
  7.2 0.7 compare_select_fusion.3
  7.9 0.7 scatter_custom_fusion
  8.6 0.7 fusion.14
  9.3 0.7 fusion.15
  10.0 20.7 %compare_select_fusion.4 = s32[256]{0:T(256)S(1)} fusion(s32[256]{0:T(256)} %param.15, s32[]{:T(128)} %bitcast, s32[]{:T(128)} %bitcast.1, s32[]{:T(128)} %bitcast.2, s32[]{:T(128)} %bitcast.3, s32[]{:T(128)} %bitcast.4, s32[]{:T(128)} %bitcast.5, s32[]{:T(128)} %bitcast.6, s32[]{:T(128)} %bitcast.7, s32[]{:T(128)} %bitcast.8, s32[]{:T(128)} %bitcast.9, ...), kind=kLoop, calls=%fused_computation.30 | loop fusion | flops 16640 | bytes 2176 | tf_op jit(solution)/shard_map/gather | solution.py:34
  31.5 0.7 compare_select_fusion.1
  32.2 0.8 gather_fusion
  33.0 6.8 %convolution_multiply_fusion.1 = f32[256,16,128]{2,1,0:T(8,128)S(1)} fusion(bf16[256,16,128]{2,1,0:T(8,128)(2,1)S(1)} %gather_fusion, bf16[256,128,128]{2,1,0:T(8,128)(2,1)} %param.14, f32[256]{0:T(256)S(1)} %compare_convert_fusion), kind=kOutput, calls=%fused_computation.7 | convolution fusion | flops 134742016 | bytes 11535360 | tf_op jit(solution)/shard_map/nfk,nrk->nfr/dot_general | solution.py:39
  39.9 9.0 %scatter_fusion = f32[32,16,128]{2,1,0:T(8,128)S(1)} fusion(f32[32,16,128]{2,1,0:T(8,128)S(1)} %broadcast_in_dim.8, s32[256]{0:T(256)S(1)} %bitcast.83, f32[256,16,128]{2,1,0:T(8,128)S(1)} %convolution_multiply_fusion.1), kind=kCustom, calls=%fused_computation.3 | custom fusion | flops 524288 | bytes 6292480 | tf_op jit(solution)/shard_map/scatter-add | solution.py:43
  48.9 0.7 copy-done.1
  49.8 29.3 %all-gather.2.cloned.1.call-done = f32[4,8,4,1,16,128]{5,4,3,2,1,0:T(8,128)} async-done(((f32[1,8,4,1,16,128]{5,4,3,2,1,0:T(8,128)}), f32[4,8,4,1,16,128]{5,4,3,2,1,0:T(8,128)}) %all-gather.2.cloned.1.call-update) | async-done | bytes 1048592 | tf_op jit(solution)/shard_map/all_gather | solution.py:46
  79.1 1.3 %reduce_sum.9 = f32[8,4,16,128]{3,2,1,0:T(8,128)S(1)} reduce(f32[4,8,4,1,16,128]{5,4,3,2,1,0:T(8,128)} %all-gather.2.cloned.1.call-done, f32[]{:T(128)} %constant.6.clone.1), dimensions={0,3}, to_apply=%region_2.0 | reduce | flops 196608 | bytes 1310724 | tf_op jit(solution)/shard_map/reduce_sum | solution.py:46
  80.4 0.6 dynamic-slice_bitcast_fusion
  81.0 4.6 %all-to-all-start = ((f32[8,1,1,16,128]{4,3,2,1,0:T(8,128)}), f32[8,1,1,16,128]{4,3,2,1,0:T(8,128)S(1)}, u32[]{:S(2)}, u32[]{:S(2)}) async-start(f32[8,1,1,16,128]{4,3,2,1,0:T(8,128)} %dynamic-slice_bitcast_fusion), calls=%async_computation | async-start | bytes 131072 | tf_op jit(solution)/shard_map/all_to_all | solution.py:49
  85.7 5.9 %all-to-all-done = f32[8,1,1,16,128]{4,3,2,1,0:T(8,128)S(1)} async-done(((f32[8,1,1,16,128]{4,3,2,1,0:T(8,128)}), f32[8,1,1,16,128]{4,3,2,1,0:T(8,128)S(1)}, u32[]{:S(2)}, u32[]{:S(2)}) %all-to-all-start) | async-done | bytes 65568 | tf_op jit(solution)/shard_map/all_to_all | solution.py:49
  91.6 0.9 multiply_convert_fusion.1
  92.5 0.8 fusion.6
  93.3 3.3 %all-to-all-start.1 = ((bf16[8,1,1,16,128]{4,3,1,2,0:T(8,128)(2,1)}), bf16[8,1,1,16,128]{4,3,1,2,0:T(8,128)(2,1)S(1)}, u32[]{:S(2)}, u32[]{:S(2)}) async-start(bf16[8,1,1,16,128]{4,3,1,2,0:T(8,128)(2,1)} %bitcast.43), calls=%async_computation.1 | async-start | bytes 65536 | tf_op jit(solution)/shard_map/all_to_all | solution.py:66
  96.6 5.7 %all-to-all-done.1 = bf16[8,1,1,16,128]{4,3,1,2,0:T(8,128)(2,1)S(1)} async-done(((bf16[8,1,1,16,128]{4,3,1,2,0:T(8,128)(2,1)}), bf16[8,1,1,16,128]{4,3,1,2,0:T(8,128)(2,1)S(1)}, u32[]{:S(2)}, u32[]{:S(2)}) %all-to-all-start.1) | async-done | bytes 32800 | tf_op jit(solution)/shard_map/all_to_all | solution.py:66
  102.3 8.9 %all_gather.7 = bf16[8,4,1,16,128]{4,3,1,0,2:T(8,128)(2,1)S(1)} all-gather(bf16[8,1,1,16,128]{4,3,1,0,2:T(8,128)(2,1)S(1)} %bitcast.81), channel_id=1, replica_groups=mesh['feat'=8,'col'=4] {'col'}, dimensions={1}, use_global_device_ids=true | all-gather | bytes 163840 | tf_op jit(solution)/shard_map/all_gather | solution.py:67
  111.2 0.8 gather_fusion.1
  112.1 4.7 %convolution_multiply_fusion = f32[256,16,128]{2,1,0:T(8,128)S(1)} fusion(bf16[256,16,128]{2,1,0:T(8,128)(2,1)S(1)} %gather_fusion.1, bf16[256,128,128]{2,1,0:T(8,128)(2,1)} %param.14, f32[256]{0:T(256)S(1)} %compare_convert_fusion), kind=kOutput, calls=%fused_computation.6 | convolution fusion | flops 134742016 | bytes 11535360 | tf_op jit(solution)/shard_map/nfr,nrk->nfk/dot_general | solution.py:71
  116.8 1.4 %fusion.2 = bf16[16,128,32]{1,2,0:T(8,128)(2,1)S(1)} fusion(f32[256,16,128]{2,1,0:T(8,128)S(1)} %convolution_multiply_fusion, s32[256]{0:T(256)S(1)} %copy-done.4), kind=kOutput, calls=%fused_computation.8 | convolution fusion | flops 201400320 | bytes 2229248 | tf_op jit(solution)/shard_map/nc,nfk->fck/dot_general | solution.py:77
  118.2 0.7 copy.32
  (29 shorter events, 0.3 us)
Async XLA Ops:
  7.2 24.3 %copy-start = (bf16[16,4096]{1,0:T(8,128)(2,1)S(1)}, bf16[16,4096]{1,0:T(8,128)(2,1)}, u32[]{:S(2)}) copy-start(bf16[16,4096]{1,0:T(8,128)(2,1)} %param.13) | copy-start | bytes 393220
  7.2 71.9 %all-gather.2.cloned.1.call-start = ((), (), s32[]{:S(2)}) async-start(), calls=%async_computation.2 | async-start | bytes 1310720 | tf_op jit(solution)/shard_map/all_gather | solution.py:46
  39.9 9.7 %copy-start.2 = (bf16[128,256]{1,0:T(8,128)(2,1)S(1)}, bf16[128,256]{1,0:T(8,128)(2,1)}, u32[]{:S(2)}) copy-start(bf16[128,256]{1,0:T(8,128)(2,1)} %param.20) | copy-start | bytes 196612
  39.9 9.7 %copy-start.3 = (bf16[128,128]{1,0:T(8,128)(2,1)S(1)}, bf16[128,128]{1,0:T(8,128)(2,1)}, u32[]{:S(2)}) copy-start(bf16[128,128]{1,0:T(8,128)(2,1)} %param.12) | copy-start | bytes 98308
  39.9 45.8 %copy-start.8 = (s32[128]{0:T(128)S(1)}, s32[128]{0:T(128)}, u32[]{:S(2)}) copy-start(s32[128]{0:T(128)} %param.19) | copy-start | bytes 1540
  48.9 0.7 copy-start.1
  48.9 42.7 %copy-start.5 = (bf16[128,256]{1,0:T(8,128)(2,1)S(1)}, bf16[128,256]{1,0:T(8,128)(2,1)}, u32[]{:S(2)}) copy-start(bf16[128,256]{1,0:T(8,128)(2,1)} %param.21) | copy-start | bytes 196612
  48.9 42.7 %copy-start.7 = (f32[256]{0:T(256)S(1)}, f32[256]{0:T(256)}, u32[]{:S(2)}) copy-start(f32[256]{0:T(256)} %param.22) | copy-start | bytes 3076
  48.9 43.6 %copy-start.6 = (bf16[128,256]{1,0:T(8,128)(2,1)S(1)}, bf16[128,256]{1,0:T(8,128)(2,1)}, u32[]{:S(2)}) copy-start(bf16[128,256]{1,0:T(8,128)(2,1)} %param.23) | copy-start | bytes 196612
  81.0 10.5 %all-to-all-start = ((f32[8,1,1,16,128]{4,3,2,1,0:T(8,128)}), f32[8,1,1,16,128]{4,3,2,1,0:T(8,128)S(1)}, u32[]{:S(2)}, u32[]{:S(2)}) async-start(f32[8,1,1,16,128]{4,3,2,1,0:T(8,128)} %dynamic-slice_bitcast_fusion), calls=%async_computation | async-start | bytes 131072 | tf_op jit(solution)/shard_map/all_to_all | solution.py:49
  93.3 9.0 %all-to-all-start.1 = ((bf16[8,1,1,16,128]{4,3,1,2,0:T(8,128)(2,1)}), bf16[8,1,1,16,128]{4,3,1,2,0:T(8,128)(2,1)S(1)}, u32[]{:S(2)}, u32[]{:S(2)}) async-start(bf16[8,1,1,16,128]{4,3,1,2,0:T(8,128)(2,1)} %bitcast.43), calls=%async_computation.1 | async-start | bytes 65536 | tf_op jit(solution)/shard_map/all_to_all | solution.py:66
  112.1 4.7 %copy-start.4 = (s32[256]{0:T(256)S(1)}, s32[256]{0:T(256)}, u32[]{:S(2)}) copy-start(s32[256]{0:T(256)} %param.16) | copy-start | bytes 3076
Sparse Core Ops, SparseCore 0:
  49.7 29.3 all-gather.1
